TPU v7x, 32 devices: a whole 2x2x4 slice. The times are simulated.
32 devices in a mesh: ctx: 4 (over z), head: 8 (over y, x, core).
Axes of the slice: x: 2, y: 2, z: 4, core: 2. Of those that a mesh axis runs over, the one named last changes fastest.
Arguments:
- layer_input: bfloat16 [1024, 4096], P(('ctx', 'head')), may hold values from -6 to 6
- w_query: bfloat16 [4096, 4096], P('ctx', 'head'), may hold values from -0.09375 to 0.09375
- w_key: bfloat16 [4096, 4096], P('ctx', 'head'), may hold values from -0.09375 to 0.09375
- w_value: bfloat16 [4096, 4096], P('ctx', 'head'), may hold values from -0.09375 to 0.09375
- w_out: bfloat16 [4096, 4096], P('head'), may hold values from -0.09375 to 0.09375
- log_decay: float32 [32, 1024], P('head', 'ctx'), may hold values from -2 to 0
- level_gain: float32 [32, 10], P('head'), may hold values from 0.5 to 2
- level_mask: int32 [8, 10], P('ctx'), may hold values 0 or 1
Outputs:
- layer_out: bfloat16 [1024, 4096], P(('ctx', 'head'))
All inputs are finite; a program needn't handle non-finite values. No bound on the sum of `level_mask` on one device may be relied on, other than what follows from the above.
Results may differ from a plain program's by a relative error of at most 0.023.
Values may be sent and summed in bfloat16 or wider, within the bound.
A program may use at most 64 MiB of HBM per device.

v0:
```python
import jax
import jax.numpy as jnp
from jax import lax
from jax.sharding import PartitionSpec as P

HEAD_DIM = 128
BLOCK = 128


def swapped(value, axis, stride):
    mask = 2**stride
    pairs = [(source, source ^ mask) for source in range(lax.axis_size(axis))]
    return lax.ppermute(value, axis, pairs)


def levels_of(first, second, count):
    mixed = jnp.bitwise_xor(first, second)
    result = jnp.zeros(mixed.shape, jnp.int32)
    for level_bit in range(count):
        result = result + (mixed >= 2**level_bit).astype(jnp.int32)
    return result


def unit_rows(block):
    floated = block.astype(jnp.float32)
    return (floated / jnp.sqrt(jnp.sum(floated * floated, axis=-1, keepdims=True) + 1e-06)).astype(
        jnp.bfloat16
    )


def on_device(layer_input, w_query, w_key, w_value, w_out, log_decay, level_gain, level_mask):
    full_query, full_key, full_value = (
        lax.all_gather(w_query, "ctx", axis=0, tiled=True),
        lax.all_gather(w_key, "ctx", axis=0, tiled=True),
        lax.all_gather(w_value, "ctx", axis=0, tiled=True),
    )
    piece = lax.all_gather(layer_input, "head", axis=0, tiled=True)
    outputs = [
        jnp.dot(piece, weight, preferred_element_type=jnp.float32).astype(jnp.bfloat16)
        for weight in (full_query, full_key, full_value)
    ]
    joined = jnp.concatenate(outputs, axis=1)
    width = full_query.shape[1]
    local_heads = width // HEAD_DIM
    span = joined.shape[0]
    query_unit = unit_rows(joined[:, :width].reshape(span, local_heads, HEAD_DIM))
    key_unit = unit_rows(joined[:, width : 2 * width].reshape(span, local_heads, HEAD_DIM))
    values = joined[:, 2 * width :].reshape(span, local_heads, HEAD_DIM)
    cum = jnp.cumsum(log_decay, axis=1)
    span_total = cum[:, -1]
    level_count = level_gain.shape[1]
    per_span = span // BLOCK
    ctx_index = lax.axis_index("ctx")
    blocks = ctx_index * per_span + jnp.arange(per_span, dtype=jnp.int32)
    level_range = jnp.arange(level_count, dtype=jnp.int32)
    near_levels = levels_of(blocks[:, None], blocks[None, :], level_count)
    near_onehot = (near_levels[..., None] == level_range).astype(jnp.float32)
    block_weight = level_mask.astype(jnp.float32)[:, None, :] * level_gain[None, :, :]
    near_block = jnp.einsum("bhl,bel->hbe", block_weight, near_onehot)
    scores = jnp.einsum("thd,shd->hts", query_unit, key_unit, preferred_element_type=jnp.float32)
    position = jnp.arange(span, dtype=jnp.int32)
    causal = position[:, None] >= position[None, :]
    spread = cum[:, :, None] - cum[:, None, :]
    decay_factor = jnp.where(causal, jnp.exp(jnp.where(causal, spread, 0.0)), 0.0)
    shaped = (scores * decay_factor).reshape(local_heads, per_span, BLOCK, per_span, BLOCK)
    near_weight = (
        (shaped * near_block[:, :, None, :, None])
        .reshape(local_heads, span, span)
        .astype(jnp.bfloat16)
    )
    near_out = jnp.einsum("hts,shd->thd", near_weight, values, preferred_element_type=jnp.float32)
    decayed_key = (
        key_unit.astype(jnp.float32) * jnp.exp(span_total[None, :] - cum.T)[:, :, None]
    ).astype(jnp.bfloat16)
    span_state = jnp.einsum("thd,the->hde", decayed_key, values, preferred_element_type=jnp.float32)
    bit_count = lax.axis_size("ctx").bit_length() - 1
    bit_range = jnp.arange(bit_count, dtype=jnp.int32)
    powers = jnp.left_shift(jnp.ones_like(bit_range), bit_range)
    group_total, group_state = (span_total, span_state)
    before = jnp.zeros_like(span_total)
    collected = []
    for bit_index in range(bit_count):
        other_total, other_state = (
            swapped(group_total.astype(jnp.bfloat16), "ctx", bit_index).astype(group_total.dtype),
            swapped(group_state.astype(jnp.bfloat16), "ctx", bit_index).astype(group_state.dtype),
        )
        upper = jnp.bitwise_and(jnp.right_shift(ctx_index, bit_index), 1) == 1
        collected.append(jnp.where(upper, jnp.exp(before)[:, None, None] * other_state, 0.0))
        lower_total = jnp.where(upper, other_total, group_total)
        higher_total = jnp.where(upper, group_total, other_total)
        lower_state = jnp.where(upper, other_state, group_state)
        higher_state = jnp.where(upper, group_state, other_state)
        group_state = jnp.exp(higher_total)[:, None, None] * lower_state + higher_state
        group_total = lower_total + higher_total
        before = before + jnp.where(upper, other_total, 0.0)
    carried = jnp.stack(collected, axis=0)
    partner = jnp.bitwise_xor(ctx_index, powers)
    far_levels = levels_of(blocks[:, None], (partner * per_span)[None, :], level_count)
    far_onehot = (far_levels[..., None] == level_range).astype(jnp.float32)
    far_block = jnp.einsum("bhl,bml->bhm", block_weight, far_onehot)
    far_tokens = jnp.repeat(far_block, BLOCK, axis=0)
    scaled = query_unit.astype(jnp.float32) * jnp.exp(cum.T)[:, :, None]
    reached = jnp.einsum("thd,mhde->thme", scaled, carried, precision=lax.Precision.HIGHEST)
    far_out = jnp.einsum("thme,thm->the", reached, far_tokens, precision=lax.Precision.HIGHEST)
    heads_out = (near_out + far_out).astype(jnp.bfloat16).reshape(span, width)
    return lax.psum_scatter(
        jnp.dot(heads_out, w_out, preferred_element_type=jnp.float32).astype(jnp.bfloat16),
        "head",
        scatter_dimension=0,
        tiled=True,
    )


def solution(mesh):
    in_specs = (
        P(("ctx", "head"), None),
        P("ctx", "head"),
        P("ctx", "head"),
        P("ctx", "head"),
        P("head", None),
        P("head", "ctx"),
        P("head", None),
        P("ctx", None),
    )
    out_specs = P(("ctx", "head"), None)
    return jax.shard_map(
        on_device, mesh=mesh, in_specs=in_specs, out_specs=out_specs, check_vma=False
    )
```

profile of v0, /device:TPU:0, one launch (start us, length us, event | category | flops | bytes accessed | tf_op | source)
XLA Modules:
  0.0 354.7 jit_solution(5729758578422168812)
XLA Ops:
  6.5 0.7 all-gather.5.cloned.1.call-update
  7.3 0.7 all-gather.9.cloned.1.call-update
  8.1 0.7 all-gather.11.cloned.1.call-update
  8.8 0.5 all-gather.7.cloned.1.call-update
  9.4 0.7 reshape.199
  10.1 1.2 reduce-window.6
  11.3 0.1 slice.12
  11.3 0.1 copy.19
  11.5 0.1 copy.20
  11.6 0.1 add_bitcast_fusion
  11.7 0.1 slice.13
  11.7 0.1 copy.39
  11.8 3.1 collective-permute-start.1
  14.9 0.7 convert_element_type.227
  15.6 0.1 fusion.73
  15.7 0.9 convolution_bitcast_fusion.2
  16.6 0.1 copy.21
  16.7 0.1 copy.24
  16.9 0.1 copy.27
  17.0 0.9 fusion.33
  17.9 0.1 broadcast_in_dim.27
  18.0 0.2 copy.40
  18.2 0.3 mul.82
  18.5 0.8 mul.83
  19.4 20.3 %all-gather.5.cloned.1.call-done = bf16[256,4096]{1,0:T(8,128)(2,1)} async-done(((bf16[32,4096]{1,0:T(8,128)(2,1)}), bf16[256,4096]{1,0:T(8,128)(2,1)}) %all-gather.5.cloned.1.call-update) | async-done | bytes 2097168 | tf_op jit(solution)/shard_map/all_gather | solution.py:37
  39.8 82.3 %all-gather.9.cloned.1.call-done = bf16[4096,512]{1,0:T(8,128)(2,1)} async-done(((bf16[1024,512]{1,0:T(8,128)(2,1)}), bf16[4096,512]{1,0:T(8,128)(2,1)}) %all-gather.9.cloned.1.call-update) | async-done | bytes 4194320 | tf_op jit(solution)/shard_map/all_gather | solution.py:33
  122.1 4.1 %fusion.7 = f32[256,512]{1,0:T(8,128)S(1)} fusion(bf16[256,4096]{1,0:T(8,128)(2,1)} %all-gather.5.cloned.1.call-done, bf16[4096,512]{1,0:T(8,128)(2,1)} %all-gather.9.cloned.1.call-done), kind=kOutput, calls=%fused_computation.13 | convolution fusion | flops 1074003968 | bytes 6815744 | tf_op jit(solution)/shard_map/dot_general | solution.py:39
  126.2 0.2 reshape.203
  126.3 76.6 %all-gather.11.cloned.1.call-done = bf16[4096,512]{1,0:T(8,128)(2,1)} async-done(((bf16[1024,512]{1,0:T(8,128)(2,1)}), bf16[4096,512]{1,0:T(8,128)(2,1)}) %all-gather.11.cloned.1.call-update) | async-done | bytes 4194320 | tf_op jit(solution)/shard_map/all_gather | solution.py:34
  202.9 4.1 %fusion.6 = f32[256,512]{1,0:T(8,128)S(1)} fusion(bf16[256,4096]{1,0:T(8,128)(2,1)} %all-gather.5.cloned.1.call-done, bf16[4096,512]{1,0:T(8,128)(2,1)} %all-gather.11.cloned.1.call-done), kind=kOutput, calls=%fused_computation.11 | convolution fusion | flops 1074003968 | bytes 6815744 | tf_op jit(solution)/shard_map/dot_general | solution.py:39
  207.0 0.2 reshape.204
  207.2 0.3 multiply_reduce_fusion
  207.5 0.3 multiply_reduce_fusion.1
  207.9 0.7 multiply_convert_fusion
  208.6 75.0 %all-gather.7.cloned.1.call-done = bf16[4096,512]{1,0:T(8,128)(2,1)} async-done(((bf16[1024,512]{1,0:T(8,128)(2,1)}), bf16[4096,512]{1,0:T(8,128)(2,1)}) %all-gather.7.cloned.1.call-update) | async-done | bytes 4194320 | tf_op jit(solution)/shard_map/all_gather | solution.py:35
  283.6 4.1 %fusion.8 = bf16[32,4,8,128]{3,2,1,0:T(8,128)(2,1)S(1)} fusion(bf16[256,4096]{1,0:T(8,128)(2,1)} %all-gather.5.cloned.1.call-done, bf16[4096,512]{1,0:T(8,128)(2,1)} %all-gather.7.cloned.1.call-done), kind=kOutput, calls=%fused_computation.15 | convolution fusion | flops 1073872896 | bytes 6553600 | tf_op jit(solution)/shard_map/dot_general | solution.py:39
  287.7 0.3 fusion.87
  288.0 0.1 collective-permute-start
  288.1 5.0 %collective-permute-done = bf16[4,128,128]{2,1,0:T(8,128)(2,1)S(1)} collective-permute-done((bf16[4,128,128]{2,1,0:T(8,128)(2,1)S(1)}, bf16[4,128,128]{2,1,0:T(8,128)(2,1)S(1)}, u32[]{:S(2)}, u32[]{:S(2)}) %collective-permute-start) | collective-permute-done | bytes 131104 | tf_op jit(solution)/shard_map/ppermute | solution.py:13
  293.1 0.1 fusion.19
  293.2 0.9 collective-permute-start.2
  294.2 0.7 multiply_bitcast_fusion
  294.9 6.4 %collective-permute-done.2 = bf16[4,128,128]{2,1,0:T(8,128)(2,1)S(1)} collective-permute-done((bf16[4,128,128]{2,1,0:T(8,128)(2,1)S(1)}, bf16[4,128,128]{2,1,0:T(8,128)(2,1)S(1)}, u32[]{:S(2)}, u32[]{:S(2)}) %collective-permute-start.2) | collective-permute-done | bytes 131104 | tf_op jit(solution)/shard_map/ppermute | solution.py:13
  301.2 0.1 select_bitcast_fusion
  301.3 1.1 fusion.3
  302.4 0.6 fusion.5
  303.0 4.8 %convolution_convert_fusion = bf16[256,4096]{1,0:T(8,128)(2,1)} fusion(bf16[256,512]{0,1:T(8,128)(2,1)S(1)} %bitcast.57, bf16[512,4096]{1,0:T(8,128)(2,1)} %param.12), kind=kOutput, calls=%fused_computation | convolution fusion | flops 1074790400 | bytes 6553600 | tf_op jit(solution)/shard_map/dot_general | solution.py:107
  307.9 40.3 %reduce-scatter.2.cloned.1.call-done = bf16[32,4096]{1,0:T(8,128)(2,1)} async-done(((bf16[256,4096]{1,0:T(8,128)(2,1)}), bf16[32,4096]{1,0:T(8,128)(2,1)}) %reduce-scatter.2.cloned.1.call-update) | async-done | bytes 262160 | tf_op jit(solution)/shard_map/reduce_scatter | solution.py:106
  (17 shorter events, 0.4 us)
Async XLA Ops:
  6.5 33.2 %all-gather.5.cloned.1.call-start = ((), (), s32[]{:S(2)}) async-start(), calls=%async_computation.1 | async-start | bytes 2359296 | tf_op jit(solution)/shard_map/all_gather | solution.py:37
  7.3 114.8 %all-gather.9.cloned.1.call-start = ((), (), s32[]{:S(2)}) async-start(), calls=%async_computation.3 | async-start | bytes 5242880 | tf_op jit(solution)/shard_map/all_gather | solution.py:33
  8.0 194.9 %all-gather.11.cloned.1.call-start = ((), (), s32[]{:S(2)}) async-start(), calls=%async_computation.4 | async-start | bytes 5242880 | tf_op jit(solution)/shard_map/all_gather | solution.py:34
  8.7 274.9 %all-gather.7.cloned.1.call-start = ((), (), s32[]{:S(2)}) async-start(), calls=%async_computation.2 | async-start | bytes 5242880 | tf_op jit(solution)/shard_map/all_gather | solution.py:35
  9.3 338.8 %reduce-scatter.2.cloned.1.call-start = ((), (), s32[]{:S(2)}) async-start(), calls=%async_computation.5 | async-start | bytes 2359296 | tf_op jit(solution)/shard_map/reduce_scatter | solution.py:106
  11.8 7.6 %collective-permute-start.1 = (bf16[4]{0:T(256)(128)(2,1)S(1)}, bf16[4]{0:T(256)(128)(2,1)S(1)}, u32[]{:S(2)}, u32[]{:S(2)}) collective-permute-start(bf16[4]{0:T(256)(128)(2,1)S(1)} %bitcast_convert_fusion), channel_id=1, source_target_pairs={{0,8},{8,0},{16,24},{24,16},{1,9},{9,1},{17,25},{25,17},{2,10},{10... | collective-permute-start | bytes 32 | tf_op jit(solution)/shard_map/ppermute | solution.py:13
  288.0 5.2 %collective-permute-start = (bf16[4,128,128]{2,1,0:T(8,128)(2,1)S(1)}, bf16[4,128,128]{2,1,0:T(8,128)(2,1)S(1)}, u32[]{:S(2)}, u32[]{:S(2)}) collective-permute-start(bf16[4,128,128]{2,1,0:T(8,128)(2,1)S(1)} %get-tuple-element.17), channel_id=1, source_target_pairs={{0,8},{8,0},{16,24},{24,16},{1,9},{9,1},{17,25},{25,17},{2,10},{10... | collective-permute-start | bytes 393224 | tf_op jit(solution)/shard_map/ppermute | solution.py:13
  293.2 8.0 %collective-permute-start.2 = (bf16[4,128,128]{2,1,0:T(8,128)(2,1)S(1)}, bf16[4,128,128]{2,1,0:T(8,128)(2,1)S(1)}, u32[]{:S(2)}, u32[]{:S(2)}) collective-permute-start(bf16[4,128,128]{2,1,0:T(8,128)(2,1)S(1)} %get-tuple-element.10), channel_id=1, source_target_pairs={{0,16},{8,24},{16,0},{24,8},{1,17},{9,25},{17,1},{25,9},{2,18},{10... | collective-permute-start | bytes 393224 | tf_op jit(solution)/shard_map/ppermute | solution.py:13
Sparse Core Ops, SparseCore 0:
  9.2 30.4 all-gather.4
  41.3 80.7 all-gather.8
  123.7 79.2 all-gather.10
  204.3 79.2 all-gather.6
  308.0 40.1 reduce-scatter.1
where the time goes:
time: 355 us
  waiting for transfers between devices  308 us (87%)
  matrix products  20.7 us (6%)
  between operations  13.3 us (4%)
  other arithmetic  4.58 us (1%)
  starting transfers between devices  4.23 us (1%)
    all_gather x1, waiting for transfers between devices, on_device(): lax.all_gather(w_query, 'ctx', axis=0, tiled=True)  82.3 us
    all_gather x1, waiting for transfers between devices, on_device(): lax.all_gather(w_key, 'ctx', axis=0, tiled=True)  76.6 us
    all_gather x1, waiting for transfers between devices, on_device(): lax.all_gather(w_value, 'ctx', axis=0, tiled=True)  75 us
    reduce_scatter x1, waiting for transfers between devices, on_device(): lax.psum_scatter(jnp.dot(heads_out, w_out, preferred_element_type=jnp.flo...  40.3 us
    all_gather x1, waiting for transfers between devices, on_device(): piece = lax.all_gather(layer_input, 'head', axis=0, tiled=True)  20.3 us
    dot_general x3, matrix products, on_device(): jnp.dot(piece, weight, preferred_element_type=jnp.float32)  12.2 us
    ppermute x3, waiting for transfers between devices, swapped(): return lax.ppermute(value, axis, pairs)  11.4 us
  transfers between devices with their start and end apart: 8, of which 7 were waited for; matrix products, arithmetic and copies ran while one was open for 5% of the time, Pallas kernels for 0%

commit v1 on v0

--- a/solution.py
+++ b/solution.py
@@ -29,18 +29,24 @@
 
 
 def on_device(layer_input, w_query, w_key, w_value, w_out, log_decay, level_gain, level_mask):
-    full_query, full_key, full_value = (
-        lax.all_gather(w_query, "ctx", axis=0, tiled=True),
-        lax.all_gather(w_key, "ctx", axis=0, tiled=True),
-        lax.all_gather(w_value, "ctx", axis=0, tiled=True),
-    )
-    piece = lax.all_gather(layer_input, "head", axis=0, tiled=True)
+    n_ctx = lax.axis_size("ctx")
+    rows, model = layer_input.shape
+    depth = w_query.shape[0]
+    slices = layer_input.reshape(rows, n_ctx, depth).transpose(1, 0, 2)
+    mine = lax.all_to_all(slices, "ctx", split_axis=0, concat_axis=0)
+    piece = lax.all_gather(mine, "head", axis=1, tiled=True)
+    tokens = piece.reshape(n_ctx * piece.shape[1], depth)
     outputs = [
-        jnp.dot(piece, weight, preferred_element_type=jnp.float32).astype(jnp.bfloat16)
-        for weight in (full_query, full_key, full_value)
+        lax.psum_scatter(
+            jnp.dot(tokens, weight, preferred_element_type=jnp.float32).astype(jnp.bfloat16),
+            "ctx",
+            scatter_dimension=0,
+            tiled=True,
+        )
+        for weight in (w_query, w_key, w_value)
     ]
     joined = jnp.concatenate(outputs, axis=1)
-    width = full_query.shape[1]
+    width = w_query.shape[1]
     local_heads = width // HEAD_DIM
     span = joined.shape[0]
     query_unit = unit_rows(joined[:, :width].reshape(span, local_heads, HEAD_DIM))

time: 355 us -> 204 us (0.57)
  waiting for transfers between devices: 308 us -> 138 us
  blocking collectives: 0 us -> 15 us
  local copies, waits for them, and re-layouts: 3.36 us -> 9 us
    all_gather x4 -> x1, waiting for transfers between devices: 254 us -> 27 us  [on_device(): piece = lax.all_gather(mine, 'head', axis=1, tiled=True)]
    reduce_scatter x0 -> x3, waiting for transfers between devices: none -> 65.3 us  [on_device(): lax.psum_scatter(jnp.dot(tokens, weight, preferred_element_type=jnp.float...]
    all_to_all x0 -> x1, blocking collectives: none -> 15 us  [on_device(): mine = lax.all_to_all(slices, 'ctx', split_axis=0, concat_axis=0)]
    ppermute x3, waiting for transfers between devices: 11.4 us -> 5.2 us  [swapped(): return lax.ppermute(value, axis, pairs)]
  transfers between devices with their start and end apart: 8 -> 8, of which waited for: 7 -> 6; matrix products, arithmetic and copies ran while one was open for 5% -> 9% of each run, Pallas kernels for 0% -> 0%
where the time goes in v1:
time: 204 us
  waiting for transfers between devices  138 us (68%)
  matrix products  18.3 us (9%)
  blocking collectives  15 us (7%)
  between operations  13.4 us (7%)
  local copies, waits for them, and re-layouts  9 us (4%)
  other arithmetic  6.99 us (3%)
  starting transfers between devices  2.76 us (1%)
    reduce_scatter x3, waiting for transfers between devices, on_device(): lax.psum_scatter(jnp.dot(tokens, weight, preferred_element_type=jnp.float...  65.3 us
    reduce_scatter x1, waiting for transfers between devices, on_device(): lax.psum_scatter(jnp.dot(heads_out, w_out, preferred_element_type=jnp.flo...  40.8 us
    all_gather x1, waiting for transfers between devices, on_device(): piece = lax.all_gather(mine, 'head', axis=1, tiled=True)  27 us
    all_to_all x1, blocking collectives, on_device(): mine = lax.all_to_all(slices, 'ctx', split_axis=0, concat_axis=0)  15 us
    dot_general x3, matrix products, on_device(): jnp.dot(tokens, weight, preferred_element_type=jnp.float32)  9.17 us
    ppermute x3, waiting for transfers between devices, swapped(): return lax.ppermute(value, axis, pairs)  5.2 us
    dot_general x1, matrix products, on_device(): jnp.dot(heads_out, w_out, preferred_element_type=jnp.float32)  4.81 us
  transfers between devices with their start and end apart: 8, of which 6 were waited for; matrix products, arithmetic and copies ran while one was open for 9% of the time, Pallas kernels for 0%

profile of v1, /device:TPU:0, one launch (start us, length us, event | category | flops | bytes accessed | tf_op | source)
XLA Modules:
  0.0 203.8 jit_solution(4086264279666701032)
XLA Ops:
  6.5 1.2 reshape.204
  7.8 0.1 copy.41
  7.9 15.0 %all_to_all.5 = bf16[4,32,1024]{2,1,0:T(8,128)(2,1)S(1)} all-to-all(bf16[4,32,1024]{2,1,0:T(8,128)(2,1)S(1)} %copy.41), channel_id=1, replica_groups=mesh['ctx'=4,'head'=8] {'ctx'}, dimensions={0} | all-to-all | bytes 524288 | tf_op jit(solution)/shard_map/all_to_all | solution.py:36
  22.9 0.9 copy.42
  23.9 27.0 %all-gather.2.cloned.1.call-done = bf16[4,256,1024]{2,0,1:T(4,128)(2,1)} async-done(((bf16[4,32,1024]{2,0,1:T(4,128)(2,1)}), bf16[4,256,1024]{2,0,1:T(4,128)(2,1)}) %all-gather.2.cloned.1.call-update) | async-done | bytes 2097168 | tf_op jit(solution)/shard_map/all_gather | solution.py:37
  50.8 2.2 %copy.43 = bf16[4,256,1024]{2,1,0:T(8,128)(2,1)S(1)} copy(bf16[4,256,1024]{2,0,1:T(4,128)(2,1)} %all-gather.2.cloned.1.call-done) | data formatting | bytes 4194304 | tf_op jit(solution)/shard_map/all_gather | solution.py:37
  53.1 2.2 %convolution_convert_fusion.1 = bf16[1024,512]{1,0:T(8,128)(2,1)} fusion(bf16[1024,1024]{1,0:T(8,128)(2,1)S(1)} %bitcast.63, bf16[1024,512]{1,0:T(8,128)(2,1)S(1)} %copy-done), kind=kOutput, calls=%fused_computation.1 | convolution fusion | flops 1074266112 | bytes 4194304 | tf_op jit(solution)/shard_map/dot_general | solution.py:41
  55.4 3.4 %convolution_convert_fusion.3 = bf16[1024,512]{1,0:T(8,128)(2,1)} fusion(bf16[1024,1024]{1,0:T(8,128)(2,1)S(1)} %bitcast.64, bf16[1024,512]{1,0:T(8,128)(2,1)} %param.11), kind=kOutput, calls=%fused_computation.3 | convolution fusion | flops 1074266112 | bytes 4194304 | tf_op jit(solution)/shard_map/dot_general | solution.py:41
  58.9 1.2 reduce-window.6
  60.2 0.1 slice.12
  60.2 0.1 copy.46
  60.4 0.1 copy.47
  60.5 0.1 add_bitcast_fusion
  60.6 0.1 slice.13
  60.6 0.1 copy.69
  60.8 1.6 collective-permute-start.1
  62.3 3.5 %convolution_convert_fusion.2 = bf16[1024,512]{1,0:T(8,128)(2,1)} fusion(bf16[1024,1024]{1,0:T(8,128)(2,1)S(1)} %bitcast.65, bf16[1024,512]{1,0:T(8,128)(2,1)} %param.9), kind=kOutput, calls=%fused_computation.2 | convolution fusion | flops 1074266112 | bytes 4194304 | tf_op jit(solution)/shard_map/dot_general | solution.py:41
  65.9 0.1 copy.51
  66.1 0.1 copy.54
  66.3 0.1 fusion.70
  66.4 0.2 fusion.30
  66.6 0.1 broadcast_in_dim.27
  66.6 0.2 copy.70
  66.8 0.2 convolution_bitcast_fusion.2
  67.0 0.1 copy.48
  67.1 0.4 mul.82
  67.5 0.8 mul.83
  68.3 0.6 iota_compare_fusion
  69.0 0.5 fusion.81
  69.5 13.3 %reduce-scatter.9.cloned.1.call-done = bf16[256,512]{1,0:T(8,128)(2,1)} async-done(((bf16[1024,512]{1,0:T(8,128)(2,1)}), bf16[256,512]{1,0:T(8,128)(2,1)}) %reduce-scatter.9.cloned.1.call-update) | async-done | bytes 262160 | tf_op jit(solution)/shard_map/reduce_scatter | solution.py:40
  82.9 1.1 reshape.212
  84.0 0.3 multiply_reduce_fusion
  84.4 1.3 multiply_convert_fusion
  85.7 25.3 %reduce-scatter.5.cloned.1.call-done = bf16[256,512]{1,0:T(8,128)(2,1)} async-done(((bf16[1024,512]{1,0:T(8,128)(2,1)}), bf16[256,512]{1,0:T(8,128)(2,1)}) %reduce-scatter.5.cloned.1.call-update) | async-done | bytes 262160 | tf_op jit(solution)/shard_map/reduce_scatter | solution.py:40
  111.0 1.2 fusion.84
  112.2 0.1 collective-permute-start
  112.3 26.7 %reduce-scatter.7.cloned.1.call-done = bf16[256,512]{1,0:T(8,128)(2,1)} async-done(((bf16[1024,512]{1,0:T(8,128)(2,1)}), bf16[256,512]{1,0:T(8,128)(2,1)}) %reduce-scatter.7.cloned.1.call-update) | async-done | bytes 262160 | tf_op jit(solution)/shard_map/reduce_scatter | solution.py:40
  139.0 1.1 reshape.211
  140.1 0.3 multiply_reduce_fusion.1
  140.5 0.8 fusion.16
  141.3 1.0 collective-permute-start.2
  142.3 1.3 multiply_bitcast_fusion
  143.6 5.2 %collective-permute-done.2 = bf16[4,128,128]{2,1,0:T(8,128)(2,1)S(1)} collective-permute-done((bf16[4,128,128]{2,1,0:T(8,128)(2,1)S(1)}, bf16[4,128,128]{2,1,0:T(8,128)(2,1)S(1)}, u32[]{:S(2)}, u32[]{:S(2)}) %collective-permute-start.2) | collective-permute-done | bytes 131104 | tf_op jit(solution)/shard_map/ppermute | solution.py:13
  148.8 0.1 select_bitcast_fusion
  148.9 1.1 fusion.3
  150.0 1.7 fusion.5
  151.6 4.8 %convolution_convert_fusion = bf16[256,4096]{1,0:T(8,128)(2,1)} fusion(bf16[256,512]{0,1:T(8,128)(2,1)S(1)} %bitcast.68, bf16[512,4096]{1,0:T(8,128)(2,1)} %param.12), kind=kOutput, calls=%fused_computation | convolution fusion | flops 1074790400 | bytes 6553600 | tf_op jit(solution)/shard_map/dot_general | solution.py:113
  156.5 40.8 %reduce-scatter.11.cloned.1.call-done = bf16[32,4096]{1,0:T(8,128)(2,1)} async-done(((bf16[256,4096]{1,0:T(8,128)(2,1)}), bf16[32,4096]{1,0:T(8,128)(2,1)}) %reduce-scatter.11.cloned.1.call-update) | async-done | bytes 262160 | tf_op jit(solution)/shard_map/reduce_scatter | solution.py:112
  (34 shorter events, 0.5 us)
Async XLA Ops:
  6.5 46.5 %copy-start = (bf16[1024,512]{1,0:T(8,128)(2,1)S(1)}, bf16[1024,512]{1,0:T(8,128)(2,1)}, u32[]{:S(2)}) copy-start(bf16[1024,512]{1,0:T(8,128)(2,1)} %param.10) | copy-start | bytes 3145732
  6.5 44.3 %all-gather.2.cloned.1.call-start = ((), (), s32[]{:S(2)}) async-start(), calls=%async_computation.5 | async-start | bytes 2359296 | tf_op jit(solution)/shard_map/all_gather | solution.py:37
  23.8 59.1 %reduce-scatter.9.cloned.1.call-start = ((), (), s32[]{:S(2)}) async-start(), calls=%async_computation.8 | async-start | bytes 1310720 | tf_op jit(solution)/shard_map/reduce_scatter | solution.py:40
  55.3 3.6 %copy-start.3 = (f32[4,256]{1,0:T(4,128)S(1)}, f32[4,256]{1,0:T(4,128)}, u32[]{:S(2)}) copy-start(f32[4,256]{1,0:T(4,128)} %param.13) | copy-start | bytes 12292
  55.4 55.6 %reduce-scatter.5.cloned.1.call-start = ((), (), s32[]{:S(2)}) async-start(), calls=%async_computation.6 | async-start | bytes 1310720 | tf_op jit(solution)/shard_map/reduce_scatter | solution.py:40
  58.9 80.1 %reduce-scatter.7.cloned.1.call-start = ((), (), s32[]{:S(2)}) async-start(), calls=%async_computation.7 | async-start | bytes 1310720 | tf_op jit(solution)/shard_map/reduce_scatter | solution.py:40
  60.8 5.5 %copy-start.4 = (s32[2,10]{1,0:T(2,128)S(1)}, s32[2,10]{1,0:T(2,128)}, u32[]{:S(2)}) copy-start(s32[2,10]{1,0:T(2,128)} %param.15) | copy-start | bytes 244
  60.8 5.6 %copy-start.5 = (f32[4,10]{1,0:T(4,128)S(1)}, f32[4,10]{1,0:T(4,128)}, u32[]{:S(2)}) copy-start(f32[4,10]{1,0:T(4,128)} %param.14) | copy-start | bytes 484
  60.8 8.2 %collective-permute-start.1 = (bf16[4]{0:T(256)(128)(2,1)S(1)}, bf16[4]{0:T(256)(128)(2,1)S(1)}, u32[]{:S(2)}, u32[]{:S(2)}) collective-permute-start(bf16[4]{0:T(256)(128)(2,1)S(1)} %bitcast_convert_fusion), channel_id=1, source_target_pairs={{0,8},{8,0},{16,24},{24,16},{1,9},{9,1},{17,25},{25,17},{2,10},{10... | collective-permute-start | bytes 32 | tf_op jit(solution)/shard_map/ppermute | solution.py:13
  65.8 131.4 %reduce-scatter.11.cloned.1.call-start = ((), (), s32[]{:S(2)}) async-start(), calls=%async_computation.9 | async-start | bytes 2359296 | tf_op jit(solution)/shard_map/reduce_scatter | solution.py:112
  112.2 28.3 %collective-permute-start = (bf16[4,128,128]{2,1,0:T(8,128)(2,1)S(1)}, bf16[4,128,128]{2,1,0:T(8,128)(2,1)S(1)}, u32[]{:S(2)}, u32[]{:S(2)}) collective-permute-start(bf16[4,128,128]{2,1,0:T(8,128)(2,1)S(1)} %get-tuple-element.17), channel_id=1, source_target_pairs={{0,8},{8,0},{16,24},{24,16},{1,9},{9,1},{17,25},{25,17},{2,10},{10... | collective-permute-start | bytes 393224 | tf_op jit(solution)/shard_map/ppermute | solution.py:13
  140.5 9.5 %copy-start.1 = (bf16[256,512]{1,0:T(8,128)(2,1)S(1)}, bf16[256,512]{1,0:T(8,128)(2,1)}, u32[]{:S(2)}) copy-start(bf16[256,512]{1,0:T(8,128)(2,1)} %reduce-scatter.5.cloned.1.call-done) | copy-start | bytes 786436
  141.3 8.7 %copy-start.2 = (pred[256,256]{1,0:T(8,128)(4,1)S(1)}, pred[256,256]{1,0:T(8,128)(4,1)}, u32[]{:S(2)}) copy-start(pred[256,256]{1,0:T(8,128)(4,1)} %iota_compare_fusion) | copy-start | bytes 196612
  141.3 7.5 %collective-permute-start.2 = (bf16[4,128,128]{2,1,0:T(8,128)(2,1)S(1)}, bf16[4,128,128]{2,1,0:T(8,128)(2,1)S(1)}, u32[]{:S(2)}, u32[]{:S(2)}) collective-permute-start(bf16[4,128,128]{2,1,0:T(8,128)(2,1)S(1)} %get-tuple-element.10), channel_id=1, source_target_pairs={{0,16},{8,24},{16,0},{24,8},{1,17},{9,25},{17,1},{25,9},{2,18},{10... | collective-permute-start | bytes 393224 | tf_op jit(solution)/shard_map/ppermute | solution.py:13
Sparse Core Ops, SparseCore 0:
  23.9 26.8 all-gather.1
  55.5 27.3 reduce-scatter.8
  85.2 25.7 reduce-scatter.4
  113.1 25.7 reduce-scatter.6
  156.6 40.6 reduce-scatter.10

commit v2 on v0

--- a/solution.py
+++ b/solution.py
@@ -1,10 +1,315 @@
+import functools
+
 import jax
 import jax.numpy as jnp
 from jax import lax
+from jax.experimental import pallas as pl
+from jax.experimental.pallas import tpu as pltpu
 from jax.sharding import PartitionSpec as P
 
 HEAD_DIM = 128
 BLOCK = 128
+MESH = pl.DeviceIdType.MESH
+
+
+def flipped(index, mask):
+    bit = 1
+    while bit <= mask:
+        if mask & bit:
+            index = index + bit - 2 * bit * ((index // bit) % 2)
+        bit *= 2
+    return index
+
+
+def subsets(bits):
+    masks = [0]
+    for bit in bits:
+        masks = masks + [mask | bit for mask in masks]
+    return masks
+
+
+def bits_of(count):
+    return [2**k for k in range(count.bit_length() - 1)]
+
+
+def visit(step, me, count):
+    after, before = count - 1 - me, me
+    extra = jnp.abs(after - before)
+    more_after = after > before
+    turn = step - extra
+    half = turn // 2
+    from_end = count - 1 - jnp.where(more_after, extra, 0) - half
+    from_start = jnp.where(more_after, 0, extra) + half
+    even = turn % 2 == 0
+    paired = jnp.where(even == more_after, from_start, from_end)
+    lone = jnp.where(more_after, count - 1 - step, step)
+    return jnp.where(step < extra, lone, paired)
+
+
+def project_kernel(
+    spans, heads, x_ref, wq_ref, wk_ref, wv_ref, out_ref,
+    xs, weight, part, inbox, total,
+    w_sem, own_sem, z_send, z_recv, g_send, g_recv, p_send, p_recv,
+):
+    me, lane = lax.axis_index("ctx"), lax.axis_index("head")
+    rows = x_ref.shape[0]
+    depth, width = weight.shape[1:]
+    bits = bits_of(heads)
+    order = [visit(step, me, spans) for step in range(spans - 1)]
+    sources = (wq_ref, wk_ref, wv_ref)
+    loads = [pltpu.make_async_copy(ref, weight.at[k], w_sem.at[k]) for k, ref in enumerate(sources)]
+
+    def columns(span):
+        return x_ref.at[:, pl.ds(pl.multiple_of(span * depth, depth), depth)]
+
+    own = pltpu.make_async_copy(columns(me), xs.at[me, lane], own_sem)
+    own.start()
+    for load in loads:
+        load.start()
+    barrier = pltpu.get_barrier_semaphore()
+    for ahead in range(1, spans):
+        pl.semaphore_signal(barrier, inc=1, device_id={"ctx": lax.rem(me + ahead, spans)}, device_id_type=MESH)
+    for bit in bits:
+        pl.semaphore_signal(barrier, inc=1, device_id={"head": flipped(lane, bit)}, device_id_type=MESH)
+    pl.semaphore_wait(barrier, spans - 1 + len(bits))
+
+    def exchange(span, source):
+        return pltpu.make_async_remote_copy(
+            src_ref=columns(span), dst_ref=xs.at[source, lane],
+            send_sem=z_send.at[span], recv_sem=z_recv.at[source],
+            device_id={"ctx": span}, device_id_type=MESH,
+        )
+
+    for span in order:
+        exchange(span, me).start()
+
+    def gather(span, mask, bit):
+        block = xs.at[span, flipped(lane, mask)]
+        return pltpu.make_async_remote_copy(
+            src_ref=block, dst_ref=block,
+            send_sem=g_send.at[span, mask | bit], recv_sem=g_recv.at[span, mask | bit],
+            device_id={"head": flipped(lane, bit)}, device_id_type=MESH,
+        )
+
+    def settled(span, mask):
+        block = xs.at[span, flipped(lane, mask)]
+        return pltpu.make_async_remote_copy(
+            src_ref=block, dst_ref=block,
+            send_sem=g_send.at[span, mask], recv_sem=g_recv.at[span, mask],
+            device_id={"head": flipped(lane, bits[0])}, device_id_type=MESH,
+        )
+
+    def to_right(span, k):
+        return pltpu.make_async_remote_copy(
+            src_ref=part.at[span, k], dst_ref=inbox.at[span, k],
+            send_sem=p_send.at[span, k], recv_sem=p_recv.at[span, k],
+            device_id={"ctx": lax.rem(me + 1, spans)}, device_id_type=MESH,
+        )
+
+    def to_left(span, k):
+        slot = jnp.where(span == me - 1, spans, span)
+        return pltpu.make_async_remote_copy(
+            src_ref=part.at[span, k], dst_ref=inbox.at[slot, k],
+            send_sem=p_send.at[span, k], recv_sem=p_recv.at[slot, k],
+            device_id={"ctx": lax.rem(me + spans - 1, spans)}, device_id_type=MESH,
+        )
+
+    def landed(slot, k):
+        pltpu.make_async_remote_copy(
+            src_ref=inbox.at[slot, k], dst_ref=inbox.at[slot, k],
+            send_sem=p_send.at[0, k], recv_sem=p_recv.at[slot, k],
+            device_id={"ctx": lax.rem(me + 1, spans)}, device_id_type=MESH,
+        ).wait_recv()
+
+    def product(span, k):
+        block = xs[span]
+        if rows % 16:
+            block = block.astype(jnp.float32)
+        block = block.reshape(heads * rows, depth).astype(jnp.bfloat16)
+        return jnp.dot(block, weight[k], preferred_element_type=jnp.float32)
+
+    queue = [me] + order
+    orders = [bits[1:] + bits[:1], bits[:0:-1] + bits[:1]]
+
+    def advance(place, phase):
+        span, path = queue[place], orders[place % 2]
+        if phase == 0:
+            if place == 0:
+                own.wait()
+            else:
+                exchange(span, span).wait_recv()
+        else:
+            for mask in subsets(path[: phase - 1]):
+                settled(span, mask | path[phase - 1]).wait_recv()
+        if phase < len(bits):
+            for mask in subsets(path[:phase]):
+                gather(span, mask, path[phase]).start()
+
+    def compute(place):
+        span = queue[place]
+        for k in range(3):
+            if place == 1:
+                loads[k].wait()
+            part[span, k] = product(span, k).astype(jnp.bfloat16)
+
+            @pl.when((span > me) & (me == 0))
+            def _():
+                to_right(span, k).start()
+
+            @pl.when((span < me) & (me == spans - 1))
+            def _():
+                to_left(span, k).start()
+
+    for wave in range(spans + len(bits)):
+        for phase in range(len(bits), -1, -1):
+            place = wave - phase
+            if 0 <= place < spans:
+                advance(place, phase)
+                if phase == len(bits) and place > 0:
+                    compute(place)
+    for k in range(3):
+        total[k] = product(me, k)
+    for span in order:
+        for k in range(3):
+
+            @pl.when((span > me) & (me > 0))
+            def _():
+                landed(span, k)
+                part[span, k] = (part[span, k].astype(jnp.float32) + inbox[span, k].astype(jnp.float32)).astype(jnp.bfloat16)
+                to_right(span, k).start()
+
+            @pl.when((span < me) & (me < spans - 1))
+            def _():
+                landed(span, k)
+                part[span, k] = (part[span, k].astype(jnp.float32) + inbox[span, k].astype(jnp.float32)).astype(jnp.bfloat16)
+                to_left(span, k).start()
+
+    for k in range(3):
+
+        @pl.when(me > 0)
+        def _():
+            landed(me, k)
+            total[k] = total[k] + inbox[me, k].astype(jnp.float32)
+
+        @pl.when(me < spans - 1)
+        def _():
+            landed(spans, k)
+            total[k] = total[k] + inbox[spans, k].astype(jnp.float32)
+
+        out_ref[k] = total[k].astype(jnp.bfloat16)
+    for span in order:
+        exchange(span, me).wait_send()
+        for k in range(3):
+            to_right(span, k).wait_send()
+    for span in queue:
+        for mask in range(1, heads):
+            settled(span, mask).wait_send()
+
+
+def project(x, w_query, w_key, w_value):
+    spans, heads = lax.axis_size("ctx"), lax.axis_size("head")
+    rows = x.shape[0]
+    depth, width = w_query.shape
+    tokens = heads * rows
+    dma = pltpu.SemaphoreType.DMA
+    hbm = pl.BlockSpec(memory_space=pl.ANY)
+    return pl.pallas_call(
+        functools.partial(project_kernel, spans, heads),
+        out_shape=jax.ShapeDtypeStruct((3, tokens, width), jnp.bfloat16),
+        in_specs=[hbm] * 4,
+        out_specs=pl.BlockSpec(memory_space=pltpu.VMEM),
+        scratch_shapes=[
+            pltpu.VMEM((spans, heads, rows, depth), jnp.bfloat16),
+            pltpu.VMEM((3, depth, width), jnp.bfloat16),
+            pltpu.VMEM((spans, 3, tokens, width), jnp.bfloat16),
+            pltpu.VMEM((spans + 1, 3, tokens, width), jnp.bfloat16),
+            pltpu.VMEM((3, tokens, width), jnp.float32),
+            dma((3,)), dma, dma((spans,)), dma((spans,)),
+            dma((spans, heads)), dma((spans, heads)),
+            dma((spans, 3)), dma((spans + 1, 3)),
+        ],
+        compiler_params=pltpu.CompilerParams(collective_id=0, has_side_effects=True),
+        name="project",
+    )(x, w_query, w_key, w_value)
+
+
+def output_kernel(heads, heads_ref, w_ref, out_ref, weight, part, inbox, w_sem, s_send, s_recv):
+    lane = lax.axis_index("head")
+    rows = out_ref.shape[0]
+    chunks, chunk = part.shape[0], part.shape[-1]
+    bits = bits_of(heads)
+    loads = [
+        pltpu.make_async_copy(w_ref.at[:, pl.ds(j * chunk, chunk)], weight.at[j], w_sem.at[j])
+        for j in range(chunks)
+    ]
+    for load in loads:
+        load.start()
+    barrier = pltpu.get_barrier_semaphore()
+    for bit in bits:
+        pl.semaphore_signal(barrier, inc=1, device_id={"head": flipped(lane, bit)}, device_id_type=MESH)
+    pl.semaphore_wait(barrier, len(bits))
+    orders = [bits[:1] + bits[1:], bits[:1] + bits[:0:-1]]
+
+    def transfer(j, phase, mask):
+        bit = orders[j % 2][phase]
+        return pltpu.make_async_remote_copy(
+            src_ref=part.at[j, flipped(lane, mask | bit)], dst_ref=inbox.at[j, phase, mask],
+            send_sem=s_send.at[j, phase, mask], recv_sem=s_recv.at[j, phase, mask],
+            device_id={"head": flipped(lane, bit)}, device_id_type=MESH,
+        )
+
+    def advance(j, phase):
+        path = orders[j % 2]
+        if phase == 0:
+            loads[j].wait()
+            product = jnp.dot(heads_ref[...], weight[j], preferred_element_type=jnp.float32)
+            part[j] = product.reshape(heads, rows, chunk).astype(jnp.bfloat16)
+        else:
+            for mask in subsets(path[phase:]):
+                transfer(j, phase - 1, mask).wait_recv()
+                place = flipped(lane, mask)
+                added = part[j, place].astype(jnp.float32) + inbox[j, phase - 1, mask].astype(jnp.float32)
+                if phase < len(bits):
+                    part[j, place] = added.astype(jnp.bfloat16)
+                else:
+                    out_ref[:, pl.ds(j * chunk, chunk)] = added.astype(jnp.bfloat16)
+        if phase < len(bits):
+            for mask in subsets(path[phase + 1 :]):
+                transfer(j, phase, mask).start()
+
+    for wave in range(chunks + len(bits)):
+        for phase in range(len(bits), -1, -1):
+            if 0 <= wave - phase < chunks:
+                advance(wave - phase, phase)
+    for j in range(chunks):
+        for phase in range(len(bits)):
+            for mask in subsets(orders[j % 2][phase + 1 :]):
+                transfer(j, phase, mask).wait_send()
+
+
+def output(heads_out, w_out):
+    heads = lax.axis_size("head")
+    tokens, width = heads_out.shape
+    model = w_out.shape[1]
+    rows = tokens // heads
+    chunks = 4
+    chunk = model // chunks
+    phases = heads.bit_length() - 1
+    dma = pltpu.SemaphoreType.DMA
+    return pl.pallas_call(
+        functools.partial(output_kernel, heads),
+        out_shape=jax.ShapeDtypeStruct((rows, model), jnp.bfloat16),
+        in_specs=[pl.BlockSpec(memory_space=pltpu.VMEM), pl.BlockSpec(memory_space=pl.ANY)],
+        out_specs=pl.BlockSpec(memory_space=pltpu.VMEM),
+        scratch_shapes=[
+            pltpu.VMEM((chunks, width, chunk), jnp.bfloat16),
+            pltpu.VMEM((chunks, heads, rows, chunk), jnp.bfloat16),
+            pltpu.VMEM((chunks, phases, heads, rows, chunk), jnp.bfloat16),
+            dma((chunks,)), dma((chunks, phases, heads)), dma((chunks, phases, heads)),
+        ],
+        compiler_params=pltpu.CompilerParams(collective_id=1, has_side_effects=True),
+        name="output",
+    )(heads_out, w_out)
 
 
 def swapped(value, axis, stride):
@@ -29,23 +334,13 @@
 
 
 def on_device(layer_input, w_query, w_key, w_value, w_out, log_decay, level_gain, level_mask):
-    full_query, full_key, full_value = (
-        lax.all_gather(w_query, "ctx", axis=0, tiled=True),
-        lax.all_gather(w_key, "ctx", axis=0, tiled=True),
-        lax.all_gather(w_value, "ctx", axis=0, tiled=True),
-    )
-    piece = lax.all_gather(layer_input, "head", axis=0, tiled=True)
-    outputs = [
-        jnp.dot(piece, weight, preferred_element_type=jnp.float32).astype(jnp.bfloat16)
-        for weight in (full_query, full_key, full_value)
-    ]
-    joined = jnp.concatenate(outputs, axis=1)
-    width = full_query.shape[1]
+    joined = project(layer_input, w_query, w_key, w_value)
+    width = w_query.shape[1]
     local_heads = width // HEAD_DIM
-    span = joined.shape[0]
-    query_unit = unit_rows(joined[:, :width].reshape(span, local_heads, HEAD_DIM))
-    key_unit = unit_rows(joined[:, width : 2 * width].reshape(span, local_heads, HEAD_DIM))
-    values = joined[:, 2 * width :].reshape(span, local_heads, HEAD_DIM)
+    span = joined.shape[1]
+    query_unit = unit_rows(joined[0].reshape(span, local_heads, HEAD_DIM))
+    key_unit = unit_rows(joined[1].reshape(span, local_heads, HEAD_DIM))
+    values = joined[2].reshape(span, local_heads, HEAD_DIM)
     cum = jnp.cumsum(log_decay, axis=1)
     span_total = cum[:, -1]
     level_count = level_gain.shape[1]
@@ -103,12 +398,7 @@
     reached = jnp.einsum("thd,mhde->thme", scaled, carried, precision=lax.Precision.HIGHEST)
     far_out = jnp.einsum("thme,thm->the", reached, far_tokens, precision=lax.Precision.HIGHEST)
     heads_out = (near_out + far_out).astype(jnp.bfloat16).reshape(span, width)
-    return lax.psum_scatter(
-        jnp.dot(heads_out, w_out, preferred_element_type=jnp.float32).astype(jnp.bfloat16),
-        "head",
-        scatter_dimension=0,
-        tiled=True,
-    )
+    return output(heads_out, w_out)
 
 
 def solution(mesh):

time: 355 us -> 131 us (0.37)
  waiting for transfers between devices: 308 us -> 5.24 us
  Pallas kernels: 0 us -> 104 us
  matrix products: 20.7 us -> 3.35 us
  between operations: 13.3 us -> 0.21 us
    all_gather x4 -> x0, waiting for transfers between devices: 254 us -> none  [the longest x1 82.3 us: on_device(): lax.all_gather(w_query, 'ctx', axis=0, tiled=True)]
    pallas_call x0 -> x2, Pallas kernels: none -> 104 us  [the longest x1 72.1 us: project(): pl.pallas_call(functools.partial(project_kernel, spans, heads), out_shape...]
    reduce_scatter x1 -> x0, waiting for transfers between devices: 40.3 us -> none  [on_device(): lax.psum_scatter(jnp.dot(heads_out, w_out, preferred_element_type=jnp.flo...]
    dot_general x4 -> x0, matrix products: 17 us -> none  [the longest x3 12.2 us: on_device(): jnp.dot(piece, weight, preferred_element_type=jnp.float32)]
    ppermute x3, waiting for transfers between devices: 11.4 us -> 5.24 us  [swapped(): return lax.ppermute(value, axis, pairs)]
  transfers between devices with their start and end apart: 8 -> 3, of which waited for: 7 -> 2; matrix products, arithmetic and copies ran while one was open for 5% -> 3% of each run, Pallas kernels for 0% -> 0%
where the time goes in v2:
time: 131 us
  Pallas kernels  104 us (79%)
  other arithmetic  6.39 us (5%)
  local copies, waits for them, and re-layouts  5.95 us (5%)
  starting transfers between devices  5.93 us (5%)
  waiting for transfers between devices  5.24 us (4%)
  matrix products  3.35 us (3%)
    pallas_call x1, Pallas kernels, project(): pl.pallas_call(functools.partial(project_kernel, spans, heads), out_shape...  72.1 us
    pallas_call x1, Pallas kernels, output(): pl.pallas_call(functools.partial(output_kernel, heads), out_shape=jax.Sha...  31.6 us
    ppermute x3, starting transfers between devices, swapped(): return lax.ppermute(value, axis, pairs)  5.93 us
    ppermute x3, waiting for transfers between devices, swapped(): return lax.ppermute(value, axis, pairs)  5.24 us
  transfers between devices with their start and end apart: 3, of which 2 were waited for; matrix products, arithmetic and copies ran while one was open for 3% of the time, Pallas kernels for 0%

profile of v2, /device:TPU:0, one launch (start us, length us, event | category | flops | bytes accessed | tf_op | source)
XLA Modules:
  0.0 130.8 jit_solution(14830859698753503254)
XLA Ops:
  0.0 0.7 reshape.193
  0.7 1.2 reduce-window.6
  1.9 0.1 slice.24
  2.0 0.1 copy.20
  2.1 0.1 copy.21
  2.2 0.1 add_bitcast_fusion
  2.3 0.1 slice.25
  2.4 0.1 copy.42
  2.5 0.1 exponential_bitcast_fusion.1
  2.6 0.1 copy.25
  2.7 72.1 %project.1 = bf16[3,256,512]{2,1,0:T(8,128)(2,1)} custom-call(bf16[32,4096]{1,0:T(8,128)(2,1)} %x_ref.1, bf16[1024,512]{1,0:T(8,128)(2,1)} %wq_ref.1, bf16[1024,512]{1,0:T(8,128)(2,1)} %wk_ref.1, bf16[1024,512]{1,0:T(8,128)(2,1)} %wv_ref.1), custom_call_target="tpu_custom_call" | custom-call | tf_op jit(solution)/shard_map/project/pallas_call | solution.py:216
  74.8 0.0 copy-start
  74.8 1.2 fusion.82
  76.1 0.0 copy-start.1
  76.1 0.2 reshape.198
  76.3 0.3 multiply_reduce_fusion
  76.7 0.1 reshape_squeeze.2
  76.7 1.3 %multiply_convert_fusion = (bf16[256,4,128]{2,1,0:T(4,128)(2,1)S(1)}, bf16[256,4,128]{2,1,0:T(4,128)(2,1)}) fusion(f32[256,4]{1,0:T(8,128)S(1)} %copy.25, f32[256,4,128]{2,1,0:T(4,128)S(1)} %reshape.198, f32[256,4]{1,0:T(8,128)S(1)} %add_sqrt_fusion), kind=kLoop, calls=%fused_computation.18 | loop fusion | flops 655360 | bytes 1056768 | tf_op jit(solution)/shard_map/convert_element_type | solution.py:369
  78.1 0.3 fusion.83
  78.3 2.9 %collective-permute-start = (bf16[4,128,128]{2,1,0:T(8,128)(2,1)S(1)}, bf16[4,128,128]{2,1,0:T(8,128)(2,1)S(1)}, u32[]{:S(2)}, u32[]{:S(2)}) collective-permute-start(bf16[4,128,128]{2,1,0:T(8,128)(2,1)S(1)} %get-tuple-element.20), channel_id=1, source_target_pairs={{0,8},{8,0},{16,24},{24,16},{1,9},{9,1},{17,25},{25,17},{2,10},{10... | collective-permute-start | bytes 393224 | tf_op jit(solution)/shard_map/ppermute | solution.py:318
  81.2 0.1 collective-permute-start.1
  81.3 0.1 copy.28
  81.4 0.2 reshape.197
  81.6 0.3 multiply_reduce_fusion.1
  82.0 0.0 copy-done
  82.1 1.3 %multiply_bitcast_fusion = (f32[256,4,128,1]{2,1,0,3:T(4,128)S(1)}, bf16[256,4,128]{2,1,0:T(4,128)(2,1)}) fusion(f32[256,4]{1,0:T(8,128)S(1)} %copy.28, f32[256,4,128]{2,1,0:T(4,128)S(1)} %reshape.197, f32[256,4]{1,0:T(8,128)S(1)} %add_sqrt_fusion.1), kind=kLoop, calls=%fused_computation.17 | loop fusion | flops 524288 | bytes 1318912 | tf_op jit(solution)/shard_map/mul | solution.py:397
  83.4 0.1 fusion.68
  83.5 0.0 copy-done.1
  83.5 0.2 fusion.28
  83.7 1.4 %collective-permute-done.1 = bf16[4]{0:T(256)(128)(2,1)S(1)} collective-permute-done((bf16[4]{0:T(256)(128)(2,1)S(1)}, bf16[4]{0:T(256)(128)(2,1)S(1)}, u32[]{:S(2)}, u32[]{:S(2)}) %collective-permute-start.1) | collective-permute-done | bytes 40 | tf_op jit(solution)/shard_map/ppermute | solution.py:318
  85.1 0.0 collective-permute-done
  85.1 0.1 fusion.16
  85.2 3.0 %collective-permute-start.2 = (bf16[4,128,128]{2,1,0:T(8,128)(2,1)S(1)}, bf16[4,128,128]{2,1,0:T(8,128)(2,1)S(1)}, u32[]{:S(2)}, u32[]{:S(2)}) collective-permute-start(bf16[4,128,128]{2,1,0:T(8,128)(2,1)S(1)} %get-tuple-element.13), channel_id=1, source_target_pairs={{0,16},{8,24},{16,0},{24,8},{1,17},{9,25},{17,1},{25,9},{2,18},{10... | collective-permute-start | bytes 393224 | tf_op jit(solution)/shard_map/ppermute | solution.py:318
  88.2 0.2 convolution_bitcast_fusion.2
  88.4 0.1 broadcast_in_dim.27
  88.4 0.2 copy.43
  88.6 0.1 copy.22
  88.7 0.4 mul.90
  89.1 0.8 mul.91
  90.0 3.8 %collective-permute-done.2 = bf16[4,128,128]{2,1,0:T(8,128)(2,1)S(1)} collective-permute-done((bf16[4,128,128]{2,1,0:T(8,128)(2,1)S(1)}, bf16[4,128,128]{2,1,0:T(8,128)(2,1)S(1)}, u32[]{:S(2)}, u32[]{:S(2)}) %collective-permute-start.2) | collective-permute-done | bytes 131104 | tf_op jit(solution)/shard_map/ppermute | solution.py:318
  93.8 0.1 select_bitcast_fusion
  93.9 1.1 fusion.3
  95.0 1.7 %fusion.5 = bf16[256,4,128]{0,2,1:T(8,128)(2,1)S(1)} fusion(f32[256,4,128]{0,2,1:T(8,128)S(1)} %fusion.3, f32[4,256,256]{2,1,0:T(8,128)S(1)} %mul.91, f32[4,256]{1,0:T(4,128)S(1)} %bitcast.42, pred[256,256]{1,0:T(8,128)(4,1)S(1)} %iota_compare_fusion, bf16[256,4,128]{2,1,0:T(4,128)(2,1)} %get-tuple-element.6, bf16[256,4,128]{2,1,0:T(4,128)(2,1)} %get-tuple-element.8, ...), kind=kOutput, calls=%fused_computation.8 | convolution fusion | flops 136052736 | bytes 2691072 | tf_op jit(solution)/shard_map/hts,shd->thd/dot_general | solution.py:366
  96.6 0.8 copy.41.heads_ref
  97.5 31.6 %output.1 = bf16[32,4096]{1,0:T(8,128)(2,1)} custom-call(bf16[256,512]{1,0:T(8,128)(2,1)} %copy.41.heads_ref, bf16[512,4096]{1,0:T(8,128)(2,1)} %w_ref.1), custom_call_target="tpu_custom_call" | custom-call | tf_op jit(solution)/shard_map/output/pallas_call | solution.py:299
  129.1 1.7 %copy.73 = bf16[32,4096]{1,0:T(8,128)(2,1)} copy(bf16[32,4096]{1,0:T(8,128)(2,1)} %output.1) | data formatting | bytes 524288
  (10 shorter events, 0.2 us)
Async XLA Ops:
  74.8 7.2 %copy-start = (s32[2,10]{1,0:T(2,128)S(1)}, s32[2,10]{1,0:T(2,128)}, u32[]{:S(2)}) copy-start(s32[2,10]{1,0:T(2,128)} %param.15) | copy-start | bytes 244
  76.1 7.4 %copy-start.1 = (f32[4,10]{1,0:T(4,128)S(1)}, f32[4,10]{1,0:T(4,128)}, u32[]{:S(2)}) copy-start(f32[4,10]{1,0:T(4,128)} %param.14) | copy-start | bytes 484
  78.3 6.7 %collective-permute-start = (bf16[4,128,128]{2,1,0:T(8,128)(2,1)S(1)}, bf16[4,128,128]{2,1,0:T(8,128)(2,1)S(1)}, u32[]{:S(2)}, u32[]{:S(2)}) collective-permute-start(bf16[4,128,128]{2,1,0:T(8,128)(2,1)S(1)} %get-tuple-element.20), channel_id=1, source_target_pairs={{0,8},{8,0},{16,24},{24,16},{1,9},{9,1},{17,25},{25,17},{2,10},{10... | collective-permute-start | bytes 393224 | tf_op jit(solution)/shard_map/ppermute | solution.py:318
  81.2 3.9 %collective-permute-start.1 = (bf16[4]{0:T(256)(128)(2,1)S(1)}, bf16[4]{0:T(256)(128)(2,1)S(1)}, u32[]{:S(2)}, u32[]{:S(2)}) collective-permute-start(bf16[4]{0:T(256)(128)(2,1)S(1)} %bitcast_convert_fusion), channel_id=1, source_target_pairs={{0,8},{8,0},{16,24},{24,16},{1,9},{9,1},{17,25},{25,17},{2,10},{10... | collective-permute-start | bytes 32 | tf_op jit(solution)/shard_map/ppermute | solution.py:318
  85.2 8.6 %collective-permute-start.2 = (bf16[4,128,128]{2,1,0:T(8,128)(2,1)S(1)}, bf16[4,128,128]{2,1,0:T(8,128)(2,1)S(1)}, u32[]{:S(2)}, u32[]{:S(2)}) collective-permute-start(bf16[4,128,128]{2,1,0:T(8,128)(2,1)S(1)} %get-tuple-element.13), channel_id=1, source_target_pairs={{0,16},{8,24},{16,0},{24,8},{1,17},{9,25},{17,1},{25,9},{2,18},{10... | collective-permute-start | bytes 393224 | tf_op jit(solution)/shard_map/ppermute | solution.py:318

commit v3 on v2

--- a/solution.py
+++ b/solution.py
@@ -233,21 +233,143 @@
     )(x, w_query, w_key, w_value)
 
 
-def output_kernel(heads, heads_ref, w_ref, out_ref, weight, part, inbox, w_sem, s_send, s_recv):
-    lane = lax.axis_index("head")
+def unit(block):
+    floated = block.astype(jnp.float32)
+    norm = jnp.sqrt(jnp.sum(floated * floated, axis=-1, keepdims=True) + 1e-06)
+    return (floated / norm).astype(jnp.bfloat16)
+
+
+def attend_kernel(
+    spans, heads, qkv_ref, cum_ref, cum_t_ref, total_ref, near_ref, far_ref, w_ref, out_ref,
+    weight, part, inbox, mixed, heads_out, query, keys, state, state_out, state_in, totals,
+    w_sem, s_send, s_recv, t_own, t_send, t_recv, g_send, g_recv,
+):
+    me, lane = lax.axis_index("ctx"), lax.axis_index("head")
     rows = out_ref.shape[0]
     chunks, chunk = part.shape[0], part.shape[-1]
-    bits = bits_of(heads)
+    local_heads, per_span = state.shape[0], qkv_ref.shape[1] // BLOCK
+    bits, span_bits = bits_of(heads), bits_of(spans)
     loads = [
         pltpu.make_async_copy(w_ref.at[:, pl.ds(j * chunk, chunk)], weight.at[j], w_sem.at[j])
         for j in range(chunks)
     ]
+    own_total = pltpu.make_async_copy(total_ref, totals.at[me], t_own)
+    own_total.start()
     for load in loads:
         load.start()
     barrier = pltpu.get_barrier_semaphore()
+    for ahead in range(1, spans):
+        pl.semaphore_signal(barrier, inc=1, device_id={"ctx": lax.rem(me + ahead, spans)}, device_id_type=MESH)
     for bit in bits:
         pl.semaphore_signal(barrier, inc=1, device_id={"head": flipped(lane, bit)}, device_id_type=MESH)
-    pl.semaphore_wait(barrier, len(bits))
+    pl.semaphore_wait(barrier, spans - 1 + len(bits))
+
+    def send_total(ahead):
+        return pltpu.make_async_remote_copy(
+            src_ref=total_ref, dst_ref=totals.at[me],
+            send_sem=t_send.at[ahead], recv_sem=t_recv.at[me],
+            device_id={"ctx": lax.rem(me + ahead, spans)}, device_id_type=MESH,
+        )
+
+    def take_total(ahead):
+        source = lax.rem(me + ahead, spans)
+        return pltpu.make_async_remote_copy(
+            src_ref=total_ref, dst_ref=totals.at[source],
+            send_sem=t_send.at[ahead], recv_sem=t_recv.at[source],
+            device_id={"ctx": source}, device_id_type=MESH,
+        )
+
+    def send_state(b, head):
+        return pltpu.make_async_remote_copy(
+            src_ref=state_out.at[b, head], dst_ref=state_in.at[b, head],
+            send_sem=g_send.at[b, head], recv_sem=g_recv.at[b, head],
+            device_id={"ctx": flipped(me, span_bits[b])}, device_id_type=MESH,
+        )
+
+    for ahead in range(1, spans):
+        send_total(ahead).start()
+
+    def lanes(head):
+        return slice(head * HEAD_DIM, (head + 1) * HEAD_DIM)
+
+    for head in range(local_heads):
+        key = unit(qkv_ref[1, :, lanes(head)])
+        keys[head] = key
+        fade = jnp.exp(total_ref[head : head + 1, :] - cum_t_ref[:, head : head + 1])
+        decayed = (key.astype(jnp.float32) * fade).astype(jnp.bfloat16)
+        state[head] = lax.dot_general(
+            decayed, qkv_ref[2, :, lanes(head)], (((0,), (0,)), ((), ())), preferred_element_type=jnp.float32
+        )
+        if span_bits:
+            state_out[0, head] = state[head].astype(jnp.bfloat16)
+            send_state(0, head).start()
+
+    def near(head):
+        query[head] = unit(qkv_ref[0, :, lanes(head)])
+        key = keys[head]
+        for a in range(per_span):
+            at = slice(a * BLOCK, (a + 1) * BLOCK)
+            near_out = None
+            for e in range(a + 1):
+                of = slice(e * BLOCK, (e + 1) * BLOCK)
+                scores = lax.dot_general(
+                    query[head, at, :], key[of, :], (((1,), (1,)), ((), ())), preferred_element_type=jnp.float32
+                )
+                spread = cum_t_ref[at, head : head + 1] - cum_ref[head : head + 1, of]
+                if e == a:
+                    causal = lax.broadcasted_iota(jnp.int32, (BLOCK, BLOCK), 0) >= lax.broadcasted_iota(
+                        jnp.int32, (BLOCK, BLOCK), 1
+                    )
+                    decay = jnp.where(causal, jnp.exp(jnp.where(causal, spread, 0.0)), 0.0)
+                else:
+                    decay = jnp.exp(spread)
+                shaped = (scores * decay * near_ref[(head * per_span + a) * per_span + e]).astype(jnp.bfloat16)
+                term = jnp.dot(shaped, qkv_ref[2, of, lanes(head)], preferred_element_type=jnp.float32)
+                near_out = term if near_out is None else near_out + term
+            mixed[head, at, :] = near_out
+
+    def group_total(place, size):
+        start = (place // size) * size
+        result = totals[start]
+        for i in range(1, size):
+            result = result + totals[start + i]
+        return result
+
+    split = (local_heads + 1) // 2
+    for head in range(split):
+        near(head)
+    own_total.wait()
+    for ahead in range(1, spans):
+        take_total(ahead).wait_recv()
+    before = jnp.zeros_like(total_ref[...])
+    for b, size in enumerate(span_bits):
+        upper = (me // size) % 2 == 1
+        other_total = group_total(flipped(me, size), size)
+        higher = jnp.exp(jnp.where(upper, group_total(me, size), other_total))
+        for head in range(local_heads):
+            send_state(b, head).wait_recv()
+            if b + 1 < len(span_bits):
+                other, held = state_in[b, head].astype(jnp.float32), state[head]
+                lower_state = jnp.where(upper, other, held)
+                higher_state = jnp.where(upper, held, other)
+                state[head] = higher[head : head + 1, :] * lower_state + higher_state
+                state_out[b + 1, head] = state[head].astype(jnp.bfloat16)
+                send_state(b + 1, head).start()
+        if b == 0:
+            for head in range(split, local_heads):
+                near(head)
+        for head in range(local_heads):
+            reach = jnp.exp(cum_t_ref[:, head : head + 1] + before[head : head + 1, :])
+            scaled = (query[head].astype(jnp.float32) * reach).astype(jnp.bfloat16)
+            far = jnp.dot(scaled, state_in[b, head], preferred_element_type=jnp.float32)
+            for a in range(per_span):
+                at = slice(a * BLOCK, (a + 1) * BLOCK)
+                gain = jnp.where(upper, far_ref[(a * local_heads + head) * len(span_bits) + b], 0.0)
+                mixed[head, at, :] = mixed[head, at, :] + far[at, :] * gain
+        before = before + jnp.where(upper, other_total, 0.0)
+    for head in range(local_heads):
+        heads_out[:, lanes(head)] = mixed[head].astype(jnp.bfloat16)
+
     orders = [bits[:1] + bits[1:], bits[:1] + bits[:0:-1]]
 
     def transfer(j, phase, mask):
@@ -262,7 +384,7 @@
         path = orders[j % 2]
         if phase == 0:
             loads[j].wait()
-            product = jnp.dot(heads_ref[...], weight[j], preferred_element_type=jnp.float32)
+            product = jnp.dot(heads_out[...], weight[j], preferred_element_type=jnp.float32)
             part[j] = product.reshape(heads, rows, chunk).astype(jnp.bfloat16)
         else:
             for mask in subsets(path[phase:]):
@@ -277,45 +399,61 @@
             for mask in subsets(path[phase + 1 :]):
                 transfer(j, phase, mask).start()
 
-    for wave in range(chunks + len(bits)):
-        for phase in range(len(bits), -1, -1):
-            if 0 <= wave - phase < chunks:
-                advance(wave - phase, phase)
+    for j in range(chunks):
+        advance(j, 0)
+    for wave in range(chunks + len(bits) - 1):
+        for phase in range(len(bits), 0, -1):
+            if 0 <= wave + 1 - phase < chunks:
+                advance(wave + 1 - phase, phase)
     for j in range(chunks):
         for phase in range(len(bits)):
             for mask in subsets(orders[j % 2][phase + 1 :]):
                 transfer(j, phase, mask).wait_send()
-
-
-def output(heads_out, w_out):
-    heads = lax.axis_size("head")
-    tokens, width = heads_out.shape
+    for ahead in range(1, spans):
+        send_total(ahead).wait_send()
+    for b in range(len(span_bits)):
+        for head in range(local_heads):
+            send_state(b, head).wait_send()
+
+
+def attend(qkv, cum, near_block, far_block, w_out):
+    spans, heads = lax.axis_size("ctx"), lax.axis_size("head")
+    tokens, width = qkv.shape[1:]
+    local_heads = cum.shape[0]
     model = w_out.shape[1]
     rows = tokens // heads
     chunks = 4
     chunk = model // chunks
-    phases = heads.bit_length() - 1
+    phases, rounds = heads.bit_length() - 1, spans.bit_length() - 1
     dma = pltpu.SemaphoreType.DMA
+    vmem = pl.BlockSpec(memory_space=pltpu.VMEM)
+    smem = pl.BlockSpec(memory_space=pltpu.SMEM)
+    totals = jnp.broadcast_to(cum[:, -1:], (local_heads, HEAD_DIM))
+    head_state = (local_heads, HEAD_DIM, HEAD_DIM)
     return pl.pallas_call(
-        functools.partial(output_kernel, heads),
+        functools.partial(attend_kernel, spans, heads),
         out_shape=jax.ShapeDtypeStruct((rows, model), jnp.bfloat16),
-        in_specs=[pl.BlockSpec(memory_space=pltpu.VMEM), pl.BlockSpec(memory_space=pl.ANY)],
-        out_specs=pl.BlockSpec(memory_space=pltpu.VMEM),
+        in_specs=[vmem, vmem, vmem, vmem, smem, smem, pl.BlockSpec(memory_space=pl.ANY)],
+        out_specs=vmem,
         scratch_shapes=[
             pltpu.VMEM((chunks, width, chunk), jnp.bfloat16),
             pltpu.VMEM((chunks, heads, rows, chunk), jnp.bfloat16),
             pltpu.VMEM((chunks, phases, heads, rows, chunk), jnp.bfloat16),
+            pltpu.VMEM((local_heads, tokens, HEAD_DIM), jnp.float32),
+            pltpu.VMEM((tokens, width), jnp.bfloat16),
+            pltpu.VMEM((local_heads, tokens, HEAD_DIM), jnp.bfloat16),
+            pltpu.VMEM((local_heads, tokens, HEAD_DIM), jnp.bfloat16),
+            pltpu.VMEM(head_state, jnp.float32),
+            pltpu.VMEM((rounds, *head_state), jnp.bfloat16),
+            pltpu.VMEM((rounds, *head_state), jnp.bfloat16),
+            pltpu.VMEM((spans, local_heads, HEAD_DIM), jnp.float32),
             dma((chunks,)), dma((chunks, phases, heads)), dma((chunks, phases, heads)),
+            dma, dma((spans,)), dma((spans,)),
+            dma((rounds, local_heads)), dma((rounds, local_heads)),
         ],
         compiler_params=pltpu.CompilerParams(collective_id=1, has_side_effects=True),
-        name="output",
-    )(heads_out, w_out)
-
-
-def swapped(value, axis, stride):
-    mask = 2**stride
-    pairs = [(source, source ^ mask) for source in range(lax.axis_size(axis))]
-    return lax.ppermute(value, axis, pairs)
+        name="attend",
+    )(qkv, cum, cum.T, totals, near_block.reshape(-1), far_block.reshape(-1), w_out)
 
 
 def levels_of(first, second, count):
@@ -326,79 +464,24 @@
     return result
 
 
-def unit_rows(block):
-    floated = block.astype(jnp.float32)
-    return (floated / jnp.sqrt(jnp.sum(floated * floated, axis=-1, keepdims=True) + 1e-06)).astype(
-        jnp.bfloat16
-    )
-
-
 def on_device(layer_input, w_query, w_key, w_value, w_out, log_decay, level_gain, level_mask):
-    joined = project(layer_input, w_query, w_key, w_value)
-    width = w_query.shape[1]
-    local_heads = width // HEAD_DIM
-    span = joined.shape[1]
-    query_unit = unit_rows(joined[0].reshape(span, local_heads, HEAD_DIM))
-    key_unit = unit_rows(joined[1].reshape(span, local_heads, HEAD_DIM))
-    values = joined[2].reshape(span, local_heads, HEAD_DIM)
+    qkv = project(layer_input, w_query, w_key, w_value)
     cum = jnp.cumsum(log_decay, axis=1)
-    span_total = cum[:, -1]
     level_count = level_gain.shape[1]
-    per_span = span // BLOCK
+    per_span = log_decay.shape[1] // BLOCK
     ctx_index = lax.axis_index("ctx")
     blocks = ctx_index * per_span + jnp.arange(per_span, dtype=jnp.int32)
     level_range = jnp.arange(level_count, dtype=jnp.int32)
+    powers = jnp.array(bits_of(lax.axis_size("ctx")), jnp.int32)
+    partner = jnp.bitwise_xor(ctx_index, powers)
+    block_weight = level_mask.astype(jnp.float32)[:, None, :] * level_gain[None, :, :]
     near_levels = levels_of(blocks[:, None], blocks[None, :], level_count)
     near_onehot = (near_levels[..., None] == level_range).astype(jnp.float32)
-    block_weight = level_mask.astype(jnp.float32)[:, None, :] * level_gain[None, :, :]
-    near_block = jnp.einsum("bhl,bel->hbe", block_weight, near_onehot)
-    scores = jnp.einsum("thd,shd->hts", query_unit, key_unit, preferred_element_type=jnp.float32)
-    position = jnp.arange(span, dtype=jnp.int32)
-    causal = position[:, None] >= position[None, :]
-    spread = cum[:, :, None] - cum[:, None, :]
-    decay_factor = jnp.where(causal, jnp.exp(jnp.where(causal, spread, 0.0)), 0.0)
-    shaped = (scores * decay_factor).reshape(local_heads, per_span, BLOCK, per_span, BLOCK)
-    near_weight = (
-        (shaped * near_block[:, :, None, :, None])
-        .reshape(local_heads, span, span)
-        .astype(jnp.bfloat16)
-    )
-    near_out = jnp.einsum("hts,shd->thd", near_weight, values, preferred_element_type=jnp.float32)
-    decayed_key = (
-        key_unit.astype(jnp.float32) * jnp.exp(span_total[None, :] - cum.T)[:, :, None]
-    ).astype(jnp.bfloat16)
-    span_state = jnp.einsum("thd,the->hde", decayed_key, values, preferred_element_type=jnp.float32)
-    bit_count = lax.axis_size("ctx").bit_length() - 1
-    bit_range = jnp.arange(bit_count, dtype=jnp.int32)
-    powers = jnp.left_shift(jnp.ones_like(bit_range), bit_range)
-    group_total, group_state = (span_total, span_state)
-    before = jnp.zeros_like(span_total)
-    collected = []
-    for bit_index in range(bit_count):
-        other_total, other_state = (
-            swapped(group_total.astype(jnp.bfloat16), "ctx", bit_index).astype(group_total.dtype),
-            swapped(group_state.astype(jnp.bfloat16), "ctx", bit_index).astype(group_state.dtype),
-        )
-        upper = jnp.bitwise_and(jnp.right_shift(ctx_index, bit_index), 1) == 1
-        collected.append(jnp.where(upper, jnp.exp(before)[:, None, None] * other_state, 0.0))
-        lower_total = jnp.where(upper, other_total, group_total)
-        higher_total = jnp.where(upper, group_total, other_total)
-        lower_state = jnp.where(upper, other_state, group_state)
-        higher_state = jnp.where(upper, group_state, other_state)
-        group_state = jnp.exp(higher_total)[:, None, None] * lower_state + higher_state
-        group_total = lower_total + higher_total
-        before = before + jnp.where(upper, other_total, 0.0)
-    carried = jnp.stack(collected, axis=0)
-    partner = jnp.bitwise_xor(ctx_index, powers)
+    near_block = jnp.sum(block_weight[:, :, None, :] * near_onehot[:, None, :, :], axis=-1)
     far_levels = levels_of(blocks[:, None], (partner * per_span)[None, :], level_count)
     far_onehot = (far_levels[..., None] == level_range).astype(jnp.float32)
-    far_block = jnp.einsum("bhl,bml->bhm", block_weight, far_onehot)
-    far_tokens = jnp.repeat(far_block, BLOCK, axis=0)
-    scaled = query_unit.astype(jnp.float32) * jnp.exp(cum.T)[:, :, None]
-    reached = jnp.einsum("thd,mhde->thme", scaled, carried, precision=lax.Precision.HIGHEST)
-    far_out = jnp.einsum("thme,thm->the", reached, far_tokens, precision=lax.Precision.HIGHEST)
-    heads_out = (near_out + far_out).astype(jnp.bfloat16).reshape(span, width)
-    return output(heads_out, w_out)
+    far_block = jnp.sum(block_weight[:, :, None, :] * far_onehot[:, None, :, :], axis=-1)
+    return attend(qkv, cum, near_block.transpose(1, 0, 2), far_block, w_out)
 
 
 def solution(mesh):

time: 131 us -> 126 us (0.962)
  Pallas kernels: 104 us -> 116 us
  starting transfers between devices: 5.93 us -> 0 us
  waiting for transfers between devices: 5.24 us -> 0 us
  matrix products: 3.35 us -> 0 us
  other arithmetic: 6.39 us -> 3.6 us
    pallas_call x1, Pallas kernels: 31.6 us -> 44 us  [attend(): pl.pallas_call(functools.partial(attend_kernel, spans, heads), out_shape=...]
    ppermute x3 -> x0, starting transfers between devices: 5.93 us -> none  [swapped(): return lax.ppermute(value, axis, pairs)]
    ppermute x3 -> x0, waiting for transfers between devices: 5.24 us -> none  [swapped(): return lax.ppermute(value, axis, pairs)]
    dot_general x5 -> x0, matrix products: 3.35 us -> none  [the longest x1 1.66 us: on_device(): jnp.einsum('hts,shd->thd', near_weight, values, preferred_element_type=jn...]
  transfers between devices with their start and end apart: 3 -> 0, of which waited for: 2 -> 0; matrix products, arithmetic and copies ran while one was open for 3% -> 0% of each run, Pallas kernels for 0% -> 0%
where the time goes in v3:
time: 126 us; the launch traced here: 125 us
  Pallas kernels  116 us (92%)
  local copies, waits for them, and re-layouts  5.61 us (4%)
  other arithmetic  3.6 us (3%)
    pallas_call x1, Pallas kernels, project(): pl.pallas_call(functools.partial(project_kernel, spans, heads), out_shape...  72 us
    pallas_call x1, Pallas kernels, attend(): pl.pallas_call(functools.partial(attend_kernel, spans, heads), out_shape=...  44 us

profile of v3, /device:TPU:0, one launch (start us, length us, event | category | flops | bytes accessed | tf_op | source)
XLA Modules:
  0.0 125.3 jit_solution(6888961680589411456)
XLA Ops:
  0.0 0.7 xor_multiply_fusion
  0.7 0.7 convert_element_type.157
  1.3 0.1 fusion.29
  1.4 0.1 compare_convert_fusion
  1.5 0.7 broadcast_multiply_fusion
  2.2 0.1 multiply_reduce_fusion
  2.3 0.1 copy.21
  2.4 0.6 reshape.148.near_ref
  3.0 0.1 copy.22
  3.1 0.7 reshape.149.far_ref
  3.8 0.7 reshape.146
  4.5 1.2 reduce-window.6
  5.7 0.1 slice.12
  5.8 0.1 copy.18
  5.9 0.1 copy.19
  6.0 0.1 broadcast_add_fusion
  6.1 0.1 copy.20
  6.2 0.0 copy-start
  6.2 0.7 broadcast_in_dim.5.total_ref
  6.9 0.7 copy.23.cum_ref
  7.6 72.0 %project.1.qkv_ref = bf16[3,256,512]{2,1,0:T(8,128)(2,1)} custom-call(bf16[32,4096]{1,0:T(8,128)(2,1)} %x_ref.1, bf16[1024,512]{1,0:T(8,128)(2,1)} %wq_ref.1, bf16[1024,512]{1,0:T(8,128)(2,1)} %wk_ref.1, bf16[1024,512]{1,0:T(8,128)(2,1)} %wv_ref.1), custom_call_target="tpu_custom_call" | custom-call | tf_op jit(solution)/shard_map/project/pallas_call | solution.py:216
  79.6 0.0 copy-done
  79.6 44.0 %attend.1 = bf16[32,4096]{1,0:T(8,128)(2,1)} custom-call(bf16[3,256,512]{2,1,0:T(8,128)(2,1)} %project.1.qkv_ref, f32[4,256]{1,0:T(4,128)} %copy.23.cum_ref, f32[256,4]{1,0:T(8,128)} %bitcast.9, f32[4,128]{1,0:T(4,128)} %broadcast_in_dim.5.total_ref, f32[16]{0:T(128)} %reshape.148.near_ref, f32[16]{0:T(128)} %reshape.149.far_ref, bf16[512,4096]{1,0:T(8,128)(2,1)} %w_ref.1), custom_call_target="tpu_custom_call" | custom-call | tf_op jit(solution)/shard_map/attend/pallas_call | solution.py:433
  123.6 1.7 %copy.25 = bf16[32,4096]{1,0:T(8,128)(2,1)} copy(bf16[32,4096]{1,0:T(8,128)(2,1)} %attend.1) | data formatting | bytes 524288
  (4 shorter events, 0.1 us)
Async XLA Ops:
  6.2 73.4 %copy-start = (f32[4,2,128]{0,2,1:T(8,128)}, f32[4,2,128]{0,2,1:T(8,128)S(1)}, u32[]{:S(2)}) copy-start(f32[4,2,128]{0,2,1:T(8,128)S(1)} %copy.20) | copy-start | bytes 12292

commit v4 on v3

--- a/solution.py
+++ b/solution.py
@@ -240,8 +240,9 @@
 
 
 def attend_kernel(
-    spans, heads, qkv_ref, cum_ref, cum_t_ref, total_ref, near_ref, far_ref, w_ref, out_ref,
+    spans, heads, qkv_ref, decay_ref, gain_ref, mask_ref, w_ref, out_ref,
     weight, part, inbox, mixed, heads_out, query, keys, state, state_out, state_in, totals,
+    cum_ref, cum_t_ref, total_ref,
     w_sem, s_send, s_recv, t_own, t_send, t_recv, g_send, g_recv,
 ):
     me, lane = lax.axis_index("ctx"), lax.axis_index("head")
@@ -253,10 +254,33 @@
         pltpu.make_async_copy(w_ref.at[:, pl.ds(j * chunk, chunk)], weight.at[j], w_sem.at[j])
         for j in range(chunks)
     ]
+    for load in loads:
+        load.start()
+    tokens = qkv_ref.shape[1]
+    earlier = lax.broadcasted_iota(jnp.int32, (tokens, tokens), 1) <= lax.broadcasted_iota(
+        jnp.int32, (tokens, tokens), 0
+    )
+    decays = decay_ref[...]
+
+    def summed(first, second):
+        return lax.dot_general(
+            first, second, (((1,), (1,)), ((), ())),
+            precision=lax.Precision.HIGHEST, preferred_element_type=jnp.float32,
+        )
+
+    cum_ref[...] = summed(decays, earlier.astype(jnp.float32))
+    cum_t_ref[...] = summed(earlier.astype(jnp.float32), decays)
+    total_ref[...] = summed(decays, jnp.ones((HEAD_DIM, tokens), jnp.float32))
+    level_count = gain_ref.shape[1]
+
+    def level_weight(head, a, mixed_blocks):
+        level = mixed_blocks.bit_length()
+        if level >= level_count:
+            return jnp.float32(0)
+        return gain_ref[head, level] * mask_ref[a, level].astype(jnp.float32)
+
     own_total = pltpu.make_async_copy(total_ref, totals.at[me], t_own)
     own_total.start()
-    for load in loads:
-        load.start()
     barrier = pltpu.get_barrier_semaphore()
     for ahead in range(1, spans):
         pl.semaphore_signal(barrier, inc=1, device_id={"ctx": lax.rem(me + ahead, spans)}, device_id_type=MESH)
@@ -323,7 +347,7 @@
                     decay = jnp.where(causal, jnp.exp(jnp.where(causal, spread, 0.0)), 0.0)
                 else:
                     decay = jnp.exp(spread)
-                shaped = (scores * decay * near_ref[(head * per_span + a) * per_span + e]).astype(jnp.bfloat16)
+                shaped = (scores * decay * level_weight(head, a, a ^ e)).astype(jnp.bfloat16)
                 term = jnp.dot(shaped, qkv_ref[2, of, lanes(head)], preferred_element_type=jnp.float32)
                 near_out = term if near_out is None else near_out + term
             mixed[head, at, :] = near_out
@@ -364,7 +388,7 @@
             far = jnp.dot(scaled, state_in[b, head], preferred_element_type=jnp.float32)
             for a in range(per_span):
                 at = slice(a * BLOCK, (a + 1) * BLOCK)
-                gain = jnp.where(upper, far_ref[(a * local_heads + head) * len(span_bits) + b], 0.0)
+                gain = jnp.where(upper, level_weight(head, a, size * per_span + a), 0.0)
                 mixed[head, at, :] = mixed[head, at, :] + far[at, :] * gain
         before = before + jnp.where(upper, other_total, 0.0)
     for head in range(local_heads):
@@ -375,8 +399,8 @@
     def transfer(j, phase, mask):
         bit = orders[j % 2][phase]
         return pltpu.make_async_remote_copy(
-            src_ref=part.at[j, flipped(lane, mask | bit)], dst_ref=inbox.at[j, phase, mask],
-            send_sem=s_send.at[j, phase, mask], recv_sem=s_recv.at[j, phase, mask],
+            src_ref=part.at[j, flipped(lane, mask | bit)], dst_ref=inbox.at[j, mask | bit],
+            send_sem=s_send.at[j, mask | bit], recv_sem=s_recv.at[j, mask | bit],
             device_id={"head": flipped(lane, bit)}, device_id_type=MESH,
         )
 
@@ -390,7 +414,7 @@
             for mask in subsets(path[phase:]):
                 transfer(j, phase - 1, mask).wait_recv()
                 place = flipped(lane, mask)
-                added = part[j, place].astype(jnp.float32) + inbox[j, phase - 1, mask].astype(jnp.float32)
+                added = part[j, place].astype(jnp.float32) + inbox[j, mask | path[phase - 1]].astype(jnp.float32)
                 if phase < len(bits):
                     part[j, place] = added.astype(jnp.bfloat16)
                 else:
@@ -416,29 +440,28 @@
             send_state(b, head).wait_send()
 
 
-def attend(qkv, cum, near_block, far_block, w_out):
+def attend(qkv, log_decay, level_gain, level_mask, w_out):
     spans, heads = lax.axis_size("ctx"), lax.axis_size("head")
     tokens, width = qkv.shape[1:]
-    local_heads = cum.shape[0]
+    local_heads = log_decay.shape[0]
     model = w_out.shape[1]
     rows = tokens // heads
-    chunks = 4
+    chunks = 8
     chunk = model // chunks
-    phases, rounds = heads.bit_length() - 1, spans.bit_length() - 1
+    rounds = spans.bit_length() - 1
     dma = pltpu.SemaphoreType.DMA
     vmem = pl.BlockSpec(memory_space=pltpu.VMEM)
     smem = pl.BlockSpec(memory_space=pltpu.SMEM)
-    totals = jnp.broadcast_to(cum[:, -1:], (local_heads, HEAD_DIM))
     head_state = (local_heads, HEAD_DIM, HEAD_DIM)
     return pl.pallas_call(
         functools.partial(attend_kernel, spans, heads),
         out_shape=jax.ShapeDtypeStruct((rows, model), jnp.bfloat16),
-        in_specs=[vmem, vmem, vmem, vmem, smem, smem, pl.BlockSpec(memory_space=pl.ANY)],
+        in_specs=[vmem, vmem, smem, smem, pl.BlockSpec(memory_space=pl.ANY)],
         out_specs=vmem,
         scratch_shapes=[
             pltpu.VMEM((chunks, width, chunk), jnp.bfloat16),
             pltpu.VMEM((chunks, heads, rows, chunk), jnp.bfloat16),
-            pltpu.VMEM((chunks, phases, heads, rows, chunk), jnp.bfloat16),
+            pltpu.VMEM((chunks, heads, rows, chunk), jnp.bfloat16),
             pltpu.VMEM((local_heads, tokens, HEAD_DIM), jnp.float32),
             pltpu.VMEM((tokens, width), jnp.bfloat16),
             pltpu.VMEM((local_heads, tokens, HEAD_DIM), jnp.bfloat16),
@@ -447,41 +470,21 @@
             pltpu.VMEM((rounds, *head_state), jnp.bfloat16),
             pltpu.VMEM((rounds, *head_state), jnp.bfloat16),
             pltpu.VMEM((spans, local_heads, HEAD_DIM), jnp.float32),
-            dma((chunks,)), dma((chunks, phases, heads)), dma((chunks, phases, heads)),
+            pltpu.VMEM((local_heads, tokens), jnp.float32),
+            pltpu.VMEM((tokens, local_heads), jnp.float32),
+            pltpu.VMEM((local_heads, HEAD_DIM), jnp.float32),
+            dma((chunks,)), dma((chunks, heads)), dma((chunks, heads)),
             dma, dma((spans,)), dma((spans,)),
             dma((rounds, local_heads)), dma((rounds, local_heads)),
         ],
         compiler_params=pltpu.CompilerParams(collective_id=1, has_side_effects=True),
         name="attend",
-    )(qkv, cum, cum.T, totals, near_block.reshape(-1), far_block.reshape(-1), w_out)
-
-
-def levels_of(first, second, count):
-    mixed = jnp.bitwise_xor(first, second)
-    result = jnp.zeros(mixed.shape, jnp.int32)
-    for level_bit in range(count):
-        result = result + (mixed >= 2**level_bit).astype(jnp.int32)
-    return result
+    )(qkv, log_decay, level_gain, level_mask, w_out)
 
 
 def on_device(layer_input, w_query, w_key, w_value, w_out, log_decay, level_gain, level_mask):
     qkv = project(layer_input, w_query, w_key, w_value)
-    cum = jnp.cumsum(log_decay, axis=1)
-    level_count = level_gain.shape[1]
-    per_span = log_decay.shape[1] // BLOCK
-    ctx_index = lax.axis_index("ctx")
-    blocks = ctx_index * per_span + jnp.arange(per_span, dtype=jnp.int32)
-    level_range = jnp.arange(level_count, dtype=jnp.int32)
-    powers = jnp.array(bits_of(lax.axis_size("ctx")), jnp.int32)
-    partner = jnp.bitwise_xor(ctx_index, powers)
-    block_weight = level_mask.astype(jnp.float32)[:, None, :] * level_gain[None, :, :]
-    near_levels = levels_of(blocks[:, None], blocks[None, :], level_count)
-    near_onehot = (near_levels[..., None] == level_range).astype(jnp.float32)
-    near_block = jnp.sum(block_weight[:, :, None, :] * near_onehot[:, None, :, :], axis=-1)
-    far_levels = levels_of(blocks[:, None], (partner * per_span)[None, :], level_count)
-    far_onehot = (far_levels[..., None] == level_range).astype(jnp.float32)
-    far_block = jnp.sum(block_weight[:, :, None, :] * far_onehot[:, None, :, :], axis=-1)
-    return attend(qkv, cum, near_block.transpose(1, 0, 2), far_block, w_out)
+    return attend(qkv, log_decay, level_gain, level_mask, w_out)
 
 
 def solution(mesh):

time: 126 us -> 128 us (1.016)
  Pallas kernels: 116 us -> 126 us
  local copies, waits for them, and re-layouts: 5.61 us -> 1.67 us
  other arithmetic: 3.6 us -> 0 us
    pallas_call x1, Pallas kernels: 44 us -> 54 us  [attend(): pl.pallas_call(functools.partial(attend_kernel, spans, heads), out_shape=...]
    reshape x3 -> x0, local copies, waits for them, and re-layouts: 1.99 us -> none
    mul x2 -> x0, other arithmetic: 1.34 us -> none  [the longest x1 0.69 us: on_device(): level_mask.astype(jnp.float32)[:, None, :] * level_gain[None, :, :]]
    another operation x3 -> x0, other arithmetic: 1.32 us -> none
where the time goes in v4:
time: 128 us
  Pallas kernels  126 us (98%)
  local copies, waits for them, and re-layouts  1.67 us (1%)
    pallas_call x1, Pallas kernels, project(): pl.pallas_call(functools.partial(project_kernel, spans, heads), out_shape...  72 us
    pallas_call x1, Pallas kernels, attend(): pl.pallas_call(functools.partial(attend_kernel, spans, heads), out_shape=...  54 us

profile of v4, /device:TPU:0, one launch (start us, length us, event | category | flops | bytes accessed | tf_op | source)
XLA Modules:
  0.0 127.8 jit_solution(13378317228884683512)
XLA Ops:
  0.0 72.0 %project.1.qkv_ref = bf16[3,256,512]{2,1,0:T(8,128)(2,1)} custom-call(bf16[32,4096]{1,0:T(8,128)(2,1)} %x_ref.1, bf16[1024,512]{1,0:T(8,128)(2,1)} %wq_ref.1, bf16[1024,512]{1,0:T(8,128)(2,1)} %wk_ref.1, bf16[1024,512]{1,0:T(8,128)(2,1)} %wv_ref.1), custom_call_target="tpu_custom_call" | custom-call | tf_op jit(solution)/shard_map/project/pallas_call | solution.py:216
  72.1 54.0 %attend.1 = bf16[32,4096]{1,0:T(8,128)(2,1)} custom-call(bf16[3,256,512]{2,1,0:T(8,128)(2,1)} %project.1.qkv_ref, f32[4,256]{1,0:T(4,128)} %decay_ref.1, f32[4,10]{1,0:T(4,128)} %gain_ref.1, s32[2,10]{1,0:T(2,128)} %mask_ref.1, bf16[512,4096]{1,0:T(8,128)(2,1)} %w_ref.1), custom_call_target="tpu_custom_call" | custom-call | tf_op jit(solution)/shard_map/attend/pallas_call | solution.py:456
  126.1 1.7 %copy.10 = bf16[32,4096]{1,0:T(8,128)(2,1)} copy(bf16[32,4096]{1,0:T(8,128)(2,1)} %attend.1) | data formatting | bytes 524288
